TPU v7x, 32 devices: a whole 2x2x4 slice. The times are simulated.
32 devices in a mesh: fiber: 16 (over z, y, core), freq: 2 (over x).
Axes of the slice: x: 2, y: 2, z: 4, core: 2. Of those that a mesh axis runs over, the one named last changes fastest.
Arguments:
- spectra: bfloat16 [2, 512, 16, 2048], P(None, 'freq', 'fiber'), may hold values from -128 to 128
- valid_mask: int32 [16, 2048], P('fiber'), may hold values 0 or 1
- pair_reach: int32 [16], replicated, may hold values from 1 to 2, as said below
Outputs:
- correlations: float32 [16, 5, 2, 128, 128], P('fiber', None, 'freq')
Inputs may be any that keep to these rules, and one draw needn't show every extreme that they name: Block b is paired with blocks b + 1 to b + pair_reach[b]; every draw holds some block with reach 1 and some with reach 2.
All inputs are finite; a program needn't handle non-finite values. No bound on the sum of `valid_mask` on one device may be relied on, other than what follows from the above.
Results may differ from a plain program's by a relative error of at most 0.0012.
Values may be sent and summed in bfloat16 or wider, within the bound.
A program may use at most 128 MiB of HBM per device.

v0:
```python
import jax
import jax.numpy as jnp
from jax import lax
from jax.sharding import PartitionSpec as P

FREQS = 512
BAND = 2
LAG_DEV = 1
first_bin = 64.0
lag_step = 24.0
transform_length = 2048.0


def shifted(block, axis, distance):
    devices = range(lax.axis_size(axis))
    route = [(i - distance, i) for i in devices if i - distance in devices]
    return lax.ppermute(block, axis, route)


def twiddles(bins, lag_count):
    lag_values = jnp.arange(lag_count, dtype=jnp.float32) * lag_step
    angle = 2.0 * jnp.pi / transform_length * lag_values[:, None] * (first_bin + bins)[None, :]
    paired = jnp.stack([jnp.cos(angle), -jnp.sin(angle)], axis=2)
    return paired.reshape(lag_count, 2 * bins.shape[0])


def left_form(block_data):
    upper_half = jnp.concatenate([block_data[0], block_data[1]], axis=1)
    lower_half = jnp.concatenate([block_data[1], -block_data[0]], axis=1)
    return jnp.stack([upper_half, lower_half], axis=1)


def right_form(block_data):
    return jnp.concatenate([block_data[0], block_data[1]], axis=1)


def correlate(left_side, right_side, factors):
    products = jnp.einsum(
        "fkwi,fwj->fkij", left_side, right_side, preferred_element_type=jnp.float32
    )
    flattened = products.reshape(2 * products.shape[0], -1)
    return jnp.dot(factors, flattened, precision=lax.Precision.HIGHEST)


def select_entry(table, position):
    positions = jnp.arange(table.shape[0], dtype=jnp.int32)
    return jnp.sum(jnp.where(positions == position, table, 0))


def spectra_from(block_data, offset):
    return shifted(block_data, "fiber", offset)


def result_from(lag_tile, offset):
    return shifted(lag_tile, "fiber", offset)


def shards(spectra, valid_mask, pair_reach):
    groups = lax.axis_size("freq")
    fibers = lax.axis_size("fiber")
    lag_count = LAG_DEV * groups
    masked = spectra * valid_mask.astype(jnp.bfloat16)
    raw_blocks = lax.all_to_all(masked, "fiber", split_axis=3, concat_axis=2, tiled=True)
    values = raw_blocks.astype(jnp.float32)
    energy = (
        lax.psum(jnp.sum(values[0] * values[0] + values[1] * values[1], axis=0), "freq") / FREQS
    )
    resident = (values / jnp.sqrt(energy + 1e-06)).astype(jnp.bfloat16)
    location = lax.axis_index("fiber")
    bin_count = resident.shape[1]
    bins = lax.axis_index("freq") * bin_count + jnp.arange(bin_count, dtype=jnp.int32)
    factors = twiddles(bins.astype(jnp.float32), lag_count)
    block = resident.shape[3]
    own_left = left_form(resident)

    def nothing(left_side, right_side, table_part):
        return jnp.zeros((lag_count, block * block), jnp.float32)

    partials = []
    for offset in range(BAND + 1):
        other = resident if offset == 0 else spectra_from(resident, -offset)
        usable = jnp.logical_and(
            offset <= select_entry(pair_reach, location), location + offset < fibers
        )
        partials.append(lax.cond(usable, correlate, nothing, own_left, right_form(other), factors))
    summed = lax.psum_scatter(jnp.stack(partials), "freq", scatter_dimension=1, tiled=True)
    forward = [summed[0]]
    backward = []
    for offset in range(1, BAND + 1):
        forward.append(summed[offset])
        backward.append(result_from(summed[offset], offset))
    tiles = []
    for lag_tile in backward[::-1]:
        shaped = lag_tile.reshape(lag_tile.shape[0], block, block)
        tiles.append(jnp.swapaxes(shaped, 1, 2))
    for lag_tile in forward:
        tiles.append(lag_tile.reshape(lag_tile.shape[0], block, block))
    return jnp.stack(tiles)[None]


def solution(mesh):
    return jax.shard_map(
        shards,
        mesh=mesh,
        in_specs=(P(None, "freq", "fiber", None), P("fiber", None), P()),
        out_specs=P("fiber", None, "freq", None, None),
        check_vma=False,
    )
```

profile of v0, /device:TPU:8, one launch (start us, length us, event | category | flops | bytes accessed | tf_op | source)
XLA Modules:
  0.0 357.9 jit_solution(4956096219900850626)
XLA Ops:
  6.5 4.8 %copy.69 = bf16[2,256,1,2048]{1,0,2,3:T(2,128)(2,1)S(1)} copy(bf16[2,256,1,2048]{3,1,2,0:T(8,128)(2,1)} %param.9) | data formatting | bytes 4194304 | tf_op args[0]
  11.4 6.9 %broadcast_multiply_fusion = bf16[2,256,1,2048]{1,0,2,3:T(2,128)(2,1)S(1)} fusion(bf16[2,256,1,2048]{1,0,2,3:T(2,128)(2,1)S(1)} %copy.69, bf16[2048]{0:T(1024)(128)(2,1)S(1)} %convert_reduce_fusion), kind=kLoop, calls=%fused_computation.23 | loop fusion | flops 1048576 | bytes 4198400 | tf_op jit(solution)/shard_map/mul | solution.py:62
  18.3 53.3 %all_to_all.4 = bf16[2,256,1,2048]{1,0,2,3:T(2,128)(2,1)S(1)} all-to-all(bf16[2,256,1,2048]{1,0,2,3:T(2,128)(2,1)S(1)} %broadcast_multiply_fusion), channel_id=1, replica_groups=mesh['fiber'=16,'freq'=2] {'fiber'}, dimensions={3} | all-to-all | bytes 4194304 | tf_op jit(solution)/shard_map/all_to_all | solution.py:63
  71.6 0.3 copy_convert_fusion
  72.0 0.3 fusion.19
  72.3 1.6 copy-done
  73.9 5.0 %psum.7 = f32[16,128]{1,0:T(8,128)S(1)} all-reduce(f32[16,128]{1,0:T(8,128)S(1)} %bitcast.99), channel_id=1, replica_groups=mesh['fiber'=16,'freq'=2] {'freq'}, use_global_device_ids=true, to_apply=%region_2.3 | all-reduce | flops 2048 | bytes 16384 | tf_op jit(solution)/shard_map/psum | solution.py:66
  78.9 4.0 %divide_convert_fusion = bf16[2,256,16,128]{1,3,2,0:T(8,128)(2,1)} fusion(f32[2,256,16,128]{1,3,2,0:T(8,128)} %bitcast.87, f32[16,128]{1,0:T(8,128)S(1)} %add_sqrt_fusion), kind=kLoop, calls=%fused_computation.13 | loop fusion | flops 2097152 | bytes 6299648 | tf_op jit(solution)/shard_map/convert_element_type | solution.py:68
  82.9 2.4 collective-permute-start
  85.3 2.7 collective-permute-start.1
  88.0 0.6 fusion.21
  90.0 0.1 multiply_cosine_fusion
  90.1 0.1 copy.71
  90.3 0.2 reshape.140
  91.1 1.3 fusion.22
  92.4 1.8 slice_bitcast_fusion.5
  94.2 0.5 pad_maximum_fusion.1
  94.6 2.4 pad_maximum_fusion
  97.1 70.2 %conditional.3 = (f32[1,2,16384]{2,1,0:T(2,128)S(1)}) conditional(s32[]{:T(128)} %convert_element_type.28, () %tuple.29, (bf16[256,2,32,128]{0,3,2,1:T(8,128)(2,1)}, bf16[256,32,128]{0,2,1:T(8,128)(2,1)S(1)}, f32[2,512]{1,0:T(2,128)S(1)}) %tuple.30), branch_computations={%region_3.4_spmd, %region_4.5_spmd} | conditional | flops 738197504 | bytes 94507048 | solution.py:85
  97.1 8.3 %copy.72 = bf16[256,2,32,128]{3,2,1,0:T(8,128)(2,1)} copy(bf16[256,2,32,128]{0,3,2,1:T(8,128)(2,1)} %get-tuple-element.107) | data formatting | bytes 8388608 | tf_op jit(solution)/shard_map
  105.4 3.4 copy.82
  108.8 14.7 %fusion.24 = f32[256,2,128,128]{3,2,1,0:T(8,128)} fusion(bf16[256,2,32,128]{3,2,1,0:T(8,128)(2,1)} %copy.72, bf16[256,32,128,1]{2,1,3,0:T(8,128)(2,1)S(1)} %copy.82), kind=kOutput, calls=%fused_computation.51 | convolution fusion | flops 536870912 | bytes 39845888 | tf_op jit(solution)/shard_map/cond/branch_1_fun/fkwi,fwj->fkij/dot_general | solution.py:38
  123.6 43.1 %fusion.3 = f32[1,2,16384]{2,1,0:T(2,128)S(1)} fusion(f32[2,512]{1,0:T(2,128)S(1)} %get-tuple-element.37, f32[64,8,128,128]{3,2,1,0:T(8,128)} %bitcast.84), kind=kOutput, calls=%fused_computation.3 | convolution fusion | flops 201326592 | bytes 33689600 | tf_op jit(solution)/shard_map/cond/branch_1_fun/dot_general | solution.py:42
  167.2 1.8 slice_bitcast_fusion.3
  169.0 0.2 pad_maximum_fusion.2
  169.2 1.8 slice_bitcast_fusion.1
  171.0 1.5 pad_maximum_fusion.3
  172.5 69.6 %conditional.4 = (f32[1,2,16384]{2,1,0:T(2,128)S(1)}) conditional(s32[]{:T(128)} %convert_element_type.34, () %tuple.31, (bf16[256,2,32,128]{0,3,2,1:T(8,128)(2,1)}, bf16[256,32,128]{0,2,1:T(8,128)(2,1)S(1)}, f32[2,512]{1,0:T(2,128)S(1)}) %tuple.32), branch_computations={%region_5.6_spmd, %region_6.7_spmd} | conditional | flops 738197504 | bytes 94507048 | solution.py:85
  172.5 8.3 %copy.74 = bf16[256,2,32,128]{3,2,1,0:T(8,128)(2,1)} copy(bf16[256,2,32,128]{0,3,2,1:T(8,128)(2,1)} %get-tuple-element.110) | data formatting | bytes 8388608 | tf_op jit(solution)/shard_map
  180.8 3.4 copy.83
  184.3 14.7 %fusion.25 = f32[256,2,128,128]{3,2,1,0:T(8,128)} fusion(bf16[256,2,32,128]{3,2,1,0:T(8,128)(2,1)} %copy.74, bf16[256,32,128,1]{2,1,3,0:T(8,128)(2,1)S(1)} %copy.83), kind=kOutput, calls=%fused_computation.52 | convolution fusion | flops 536870912 | bytes 39845888 | tf_op jit(solution)/shard_map/cond/branch_1_fun/fkwi,fwj->fkij/dot_general | solution.py:38
  199.0 42.9 %fusion.9 = f32[1,2,16384]{2,1,0:T(2,128)S(1)} fusion(f32[2,512]{1,0:T(2,128)S(1)} %get-tuple-element.40, f32[64,8,128,128]{3,2,1,0:T(8,128)} %bitcast.85), kind=kOutput, calls=%fused_computation.7 | convolution fusion | flops 201326592 | bytes 33689600 | tf_op jit(solution)/shard_map/cond/branch_1_fun/dot_general | solution.py:42
  242.1 69.4 %conditional.5 = (f32[1,2,16384]{2,1,0:T(2,128)S(1)}) conditional(s32[]{:T(128)} %convert_element_type.35, () %tuple.33, (bf16[256,2,32,128]{0,3,2,1:T(8,128)(2,1)}, bf16[256,32,128]{0,2,1:T(8,128)(2,1)}, f32[2,512]{1,0:T(2,128)S(1)}) %tuple.34), branch_computations={%region_7.8_spmd, %region_8.9_spmd} | conditional | flops 738197504 | bytes 86118408 | solution.py:85
  242.2 8.0 %copy.76 = bf16[256,2,32,128]{3,2,1,0:T(8,128)(2,1)} copy(bf16[256,2,32,128]{0,3,2,1:T(8,128)(2,1)} %get-tuple-element.113) | data formatting | bytes 8388608 | tf_op jit(solution)/shard_map
  250.1 3.4 copy.84
  253.6 14.7 %fusion.26 = f32[256,2,128,128]{3,2,1,0:T(8,128)} fusion(bf16[256,2,32,128]{3,2,1,0:T(8,128)(2,1)} %copy.76, bf16[256,32,128,1]{2,1,3,0:T(8,128)(2,1)S(1)} %copy.84), kind=kOutput, calls=%fused_computation.53 | convolution fusion | flops 536870912 | bytes 39845888 | tf_op jit(solution)/shard_map/cond/branch_1_fun/fkwi,fwj->fkij/dot_general | solution.py:38
  268.3 43.0 %fusion.15 = f32[1,2,16384]{2,1,0:T(2,128)S(1)} fusion(f32[2,512]{1,0:T(2,128)S(1)} %get-tuple-element.43, f32[64,8,128,128]{3,2,1,0:T(8,128)} %bitcast.86), kind=kOutput, calls=%fused_computation.11 | convolution fusion | flops 201326592 | bytes 33689600 | tf_op jit(solution)/shard_map/cond/branch_1_fun/dot_general | solution.py:42
  311.6 0.9 pad_maximum_fusion.4
  312.5 0.6 dynamic-slice
  313.1 25.0 %all-reduce.3.cloned.1.call-done = f32[3,2,16384]{2,1,0:T(2,128)} async-done(((f32[3,2,16384]{2,1,0:T(2,128)}), f32[3,2,16384]{2,1,0:T(2,128)}) %all-reduce.3.cloned.1.call-update) | async-done | bytes 393232
  338.1 1.9 constant_dynamic-slice_fusion.2
  339.9 3.4 collective-permute-start.2
  343.3 1.9 collective-permute-start.3
  345.4 0.1 copy.79
  345.5 0.1 copy.80
  345.6 1.4 collective-permute-done.2
  347.0 2.8 collective-permute-done.3
  349.9 0.9 copy.81
  (26 shorter events, 0.2 us)
Async XLA Ops:
  6.5 4.8 %copy-start.3 = (s32[1,2048]{1,0:T(1,128)S(1)}, s32[1,2048]{1,0:T(1,128)}, u32[]{:S(2)}) copy-start(s32[1,2048]{1,0:T(1,128)} %param.10) | copy-start | bytes 24580
  6.5 331.5 %all-reduce.3.cloned.1.call-start = ((), (), s32[]{:S(2)}) async-start(), calls=%async_computation.1 | async-start | bytes 786432
  72.0 1.9 copy-start
  78.9 9.1 %copy-start.4 = (s32[16]{0:T(128)S(1)}, s32[16]{0:T(128)}, u32[]{:S(2)}) copy-start(s32[16]{0:T(128)} %param.11) | copy-start | bytes 196
  82.9 84.4 %collective-permute-start = (bf16[2,256,16,128]{1,3,2,0:T(8,128)(2,1)}, bf16[2,256,16,128]{1,3,2,0:T(8,128)(2,1)}, u32[]{:S(2)}, u32[]{:S(2)}) collective-permute-start(bf16[2,256,16,128]{1,3,2,0:T(8,128)(2,1)} %divide_convert_fusion), channel_id=1, source_target_pairs={{2,0},{4,2},{6,4},{8,6},{10,8},{12,10},{14,12},{16,14},{18,16},{20... | collective-permute-start | bytes 6291464 | tf_op jit(solution)/shard_map/ppermute | solution.py:17
  85.3 83.9 %collective-permute-start.1 = (bf16[2,256,16,128]{1,3,2,0:T(8,128)(2,1)}, bf16[2,256,16,128]{1,3,2,0:T(8,128)(2,1)}, u32[]{:S(2)}, u32[]{:S(2)}) collective-permute-start(bf16[2,256,16,128]{1,3,2,0:T(8,128)(2,1)} %divide_convert_fusion), channel_id=1, source_target_pairs={{4,0},{6,2},{8,4},{10,6},{12,8},{14,10},{16,12},{18,14},{20,16},{2... | collective-permute-start | bytes 6291464 | tf_op jit(solution)/shard_map/ppermute | solution.py:17
  97.1 8.3 %copy-start.2 = (bf16[256,32,128]{0,2,1:T(8,128)(2,1)}, bf16[256,32,128]{0,2,1:T(8,128)(2,1)S(1)}, u32[]{:S(2)}) copy-start(bf16[256,32,128]{0,2,1:T(8,128)(2,1)S(1)} %get-tuple-element.108) | copy-start | bytes 6291460 | tf_op jit(solution)/shard_map/cond
  172.5 8.3 %copy-start.1 = (bf16[256,32,128]{0,2,1:T(8,128)(2,1)}, bf16[256,32,128]{0,2,1:T(8,128)(2,1)S(1)}, u32[]{:S(2)}) copy-start(bf16[256,32,128]{0,2,1:T(8,128)(2,1)S(1)} %get-tuple-element.111) | copy-start | bytes 6291460 | tf_op jit(solution)/shard_map/cond
  242.1 70.4 %copy-start.5 = (u32[32]{0:T(128)S(1)}, u32[32]{0:T(128)}, u32[]{:S(2)}) copy-start(u32[32]{0:T(128)} %constant.41) | copy-start | bytes 388
  339.9 7.1 %collective-permute-start.2 = (f32[1,16384]{1,0:T(1,128)S(1)}, f32[1,16384]{1,0:T(1,128)S(1)}, u32[]{:S(2)}, u32[]{:S(2)}) collective-permute-start(f32[1,16384]{1,0:T(1,128)S(1)} %bitcast.94), channel_id=1, source_target_pairs={{0,4},{2,6},{4,8},{6,10},{8,12},{10,14},{12,16},{14,18},{16,20},{1... | collective-permute-start | bytes 196616 | tf_op jit(solution)/shard_map/ppermute | solution.py:17
  343.3 6.5 %collective-permute-start.3 = (f32[1,16384]{1,0:T(1,128)S(1)}, f32[1,16384]{1,0:T(1,128)S(1)}, u32[]{:S(2)}, u32[]{:S(2)}) collective-permute-start(f32[1,16384]{1,0:T(1,128)S(1)} %bitcast.92), channel_id=1, source_target_pairs={{0,2},{2,4},{4,6},{6,8},{8,10},{10,12},{12,14},{14,16},{16,18},{18... | collective-permute-start | bytes 196616 | tf_op jit(solution)/shard_map/ppermute | solution.py:17
Sparse Core Ops, SparseCore 0:
  312.6 25.3 all-reduce.2
where the time goes:
time: 365 us; the launch traced here: 358 us
  matrix products  173 us (47%)
  blocking collectives  58.2 us (16%)
  local copies, waits for them, and re-layouts  50.6 us (14%)
  waiting for transfers between devices  29.2 us (8%)
  other arithmetic  19.2 us (5%)
  between operations  16 us (4%)
  starting transfers between devices  10.4 us (3%)
    dot_general x3, matrix products, correlate(): return jnp.dot(factors, flattened, precision=lax.Precision.HIGHEST)  129 us
    all_to_all x1, blocking collectives, shards(): lax.all_to_all(masked, 'fiber', split_axis=3, concat_axis=2, tiled=True)  53.3 us
    dot_general x3, matrix products, correlate(): jnp.einsum('fkwi,fwj->fkij', left_side, right_side, preferred_element_typ...  44.1 us
    another operation x6, local copies, waits for them, and re-layouts  34.9 us
    unnamed x2, waiting for transfers between devices  25 us
    ppermute x4, starting transfers between devices, shifted(): return lax.ppermute(block, axis, route)  10.4 us
  transfers between devices with their start and end apart: 5, of which 3 were waited for; matrix products, arithmetic and copies ran while one was open for 22% of the time, Pallas kernels for 0%

commit v1 on v0

--- a/solution.py
+++ b/solution.py
@@ -60,7 +60,10 @@
     fibers = lax.axis_size("fiber")
     lag_count = LAG_DEV * groups
     masked = spectra * valid_mask.astype(jnp.bfloat16)
-    raw_blocks = lax.all_to_all(masked, "fiber", split_axis=3, concat_axis=2, tiled=True)
+    raw_blocks = jnp.concatenate(
+        lax.all_to_all(jnp.stack(jnp.split(masked, lax.axis_size("fiber"), axis=3)), "fiber", 0, 0),
+        axis=2,
+    )
     values = raw_blocks.astype(jnp.float32)
     energy = (
         lax.psum(jnp.sum(values[0] * values[0] + values[1] * values[1], axis=0), "freq") / FREQS

time: 365 us -> 321 us (0.88)
  local copies, waits for them, and re-layouts: 50.6 us -> 10.1 us
  other arithmetic: 19.2 us -> 12.8 us
  matrix products: 173 us -> 177 us
    another operation x6 -> x1, local copies, waits for them, and re-layouts: 34.9 us -> 0.05 us  [shards(): jnp.stack(jnp.split(masked, lax.axis_size('fiber'), axis=3))]
    unnamed x14 -> x24, local copies, waits for them, and re-layouts: 7.04 us -> 1.38 us
    mul x1, other arithmetic: 6.92 us -> 1.73 us  [shards(): masked = spectra * valid_mask.astype(jnp.bfloat16)]
    dot_general x3, matrix products: 44.1 us -> 48 us  [correlate(): jnp.einsum('fkwi,fwj->fkij', left_side, right_side, preferred_element_typ...]
where the time goes in v1:
time: 321 us; the launch traced here: 315 us
  matrix products  177 us (55%)
  blocking collectives  58.3 us (18%)
  waiting for transfers between devices  29.2 us (9%)
  between operations  16 us (5%)
  other arithmetic  12.8 us (4%)
  starting transfers between devices  10.4 us (3%)
  local copies, waits for them, and re-layouts  10.1 us (3%)
    dot_general x3, matrix products, correlate(): return jnp.dot(factors, flattened, precision=lax.Precision.HIGHEST)  129 us
    all_to_all x1, blocking collectives, shards(): lax.all_to_all(jnp.stack(jnp.split(masked, lax.axis_size('fiber'), axis=3...  53.3 us
    dot_general x3, matrix products, correlate(): jnp.einsum('fkwi,fwj->fkij', left_side, right_side, preferred_element_typ...  48 us
    unnamed x2, waiting for transfers between devices  25 us
    ppermute x4, starting transfers between devices, shifted(): return lax.ppermute(block, axis, route)  10.4 us
  transfers between devices with their start and end apart: 5, of which 3 were waited for; matrix products, arithmetic and copies ran while one was open for 22% of the time, Pallas kernels for 0%

profile of v1, /device:TPU:8, one launch (start us, length us, event | category | flops | bytes accessed | tf_op | source)
XLA Modules:
  0.0 315.0 jit_solution(11742878786791450981)
XLA Ops:
  6.5 0.7 convert_reduce_fusion
  7.3 1.7 bitcast_multiply_fusion
  9.2 0.1 fusion.42
  9.3 0.1 fusion.41
  9.3 0.1 fusion.40
  9.4 0.1 fusion.39
  9.6 0.1 fusion.34
  9.7 0.1 fusion.33
  9.8 53.3 %all_to_all.5 = bf16[16,2,256,1,128]{4,2,1,3,0:T(8,128)(2,1)S(1)} all-to-all(bf16[16,2,256,1,128]{4,2,1,3,0:T(8,128)(2,1)S(1)} %fusion.31), channel_id=1, replica_groups=mesh['fiber'=16,'freq'=2] {'fiber'}, dimensions={0} | all-to-all | bytes 4194304 | tf_op jit(solution)/shard_map/all_to_all | solution.py:64
  63.1 0.5 convert_bitcast_fusion.1
  63.6 0.3 fusion.30
  63.9 5.0 %psum.7 = f32[16,128]{1,0:T(8,128)S(1)} all-reduce(f32[16,128]{1,0:T(8,128)S(1)} %fusion.30), channel_id=1, replica_groups=mesh['fiber'=16,'freq'=2] {'freq'}, use_global_device_ids=true, to_apply=%region_2.3 | all-reduce | flops 2048 | bytes 16384 | tf_op jit(solution)/shard_map/psum | solution.py:69
  68.9 1.9 fusion.28
  70.8 2.4 collective-permute-start
  73.3 2.7 collective-permute-start.1
  76.0 0.6 fusion.48
  78.0 0.1 multiply_cosine_fusion
  78.1 0.1 copy.82
  78.2 0.2 reshape.136
  79.1 1.4 fusion.49
  80.5 1.8 slice_bitcast_fusion.5
  82.2 0.5 pad_maximum_fusion.1
  82.7 2.4 pad_maximum_fusion
  85.1 59.6 %conditional.3 = (f32[1,2,16384]{2,1,0:T(2,128)S(1)}) conditional(s32[]{:T(128)} %convert_element_type.31, () %tuple.29, (bf16[256,2,32,128]{3,0,2,1:T(8,128)(2,1)}, bf16[256,32,128]{2,0,1:T(8,128)(2,1)S(1)}, f32[2,512]{1,0:T(2,128)S(1)}) %tuple.30), branch_computations={%region_3.4_spmd, %region_4.5_spmd} | conditional | flops 738197504 | bytes 73535496 | solution.py:88
  85.1 16.0 %fusion.6 = f32[256,2,128,128]{3,2,1,0:T(8,128)} fusion(bf16[256,2,32,128]{3,0,2,1:T(8,128)(2,1)} %get-tuple-element.89, bf16[256,32,128,1]{2,0,1,3:T(8,128)(2,1)S(1)} %bitcast.162), kind=kOutput, calls=%fused_computation.4 | convolution fusion | flops 536870912 | bytes 39845888 | tf_op jit(solution)/shard_map/cond/branch_1_fun/fkwi,fwj->fkij/dot_general | solution.py:38
  101.1 43.1 %fusion.3 = f32[1,2,16384]{2,1,0:T(2,128)S(1)} fusion(f32[2,512]{1,0:T(2,128)S(1)} %get-tuple-element.37, f32[64,8,128,128]{3,2,1,0:T(8,128)} %bitcast.157), kind=kOutput, calls=%fused_computation.3 | convolution fusion | flops 201326592 | bytes 33689600 | tf_op jit(solution)/shard_map/cond/branch_1_fun/dot_general | solution.py:42
  144.8 1.8 slice_bitcast_fusion.3
  146.6 1.5 pad_maximum_fusion.2
  148.1 1.8 slice_bitcast_fusion.1
  149.9 0.2 pad_maximum_fusion.3
  150.1 59.2 %conditional.4 = (f32[1,2,16384]{2,1,0:T(2,128)S(1)}) conditional(s32[]{:T(128)} %convert_element_type.38, () %tuple.31, (bf16[256,2,32,128]{3,0,2,1:T(8,128)(2,1)}, bf16[256,32,128]{2,0,1:T(8,128)(2,1)}, f32[2,512]{1,0:T(2,128)S(1)}) %tuple.32), branch_computations={%region_5.6_spmd, %region_6.7_spmd} | conditional | flops 738197504 | bytes 73535496 | solution.py:88
  150.1 16.0 %fusion.15 = f32[256,2,128,128]{3,2,1,0:T(8,128)} fusion(bf16[256,2,32,128]{3,0,2,1:T(8,128)(2,1)} %get-tuple-element.92, bf16[256,32,128,1]{2,0,1,3:T(8,128)(2,1)} %bitcast.161), kind=kOutput, calls=%fused_computation.11 | convolution fusion | flops 536870912 | bytes 39845888 | tf_op jit(solution)/shard_map/cond/branch_1_fun/fkwi,fwj->fkij/dot_general | solution.py:38
  166.1 42.9 %fusion.12 = f32[1,2,16384]{2,1,0:T(2,128)S(1)} fusion(f32[2,512]{1,0:T(2,128)S(1)} %get-tuple-element.40, f32[64,8,128,128]{3,2,1,0:T(8,128)} %bitcast.158), kind=kOutput, calls=%fused_computation.10 | convolution fusion | flops 201326592 | bytes 33689600 | tf_op jit(solution)/shard_map/cond/branch_1_fun/dot_general | solution.py:42
  209.3 59.3 %conditional.5 = (f32[1,2,16384]{2,1,0:T(2,128)S(1)}) conditional(s32[]{:T(128)} %convert_element_type.39, () %tuple.33, (bf16[256,2,32,128]{3,0,2,1:T(8,128)(2,1)}, bf16[256,32,128]{2,0,1:T(8,128)(2,1)S(1)}, f32[2,512]{1,0:T(2,128)S(1)}) %tuple.34), branch_computations={%region_7.8_spmd, %region_8.9_spmd} | conditional | flops 738197504 | bytes 73535496 | solution.py:88
  209.3 16.0 %fusion.24 = f32[256,2,128,128]{3,2,1,0:T(8,128)} fusion(bf16[256,2,32,128]{3,0,2,1:T(8,128)(2,1)} %get-tuple-element.95, bf16[256,32,128,1]{2,0,1,3:T(8,128)(2,1)S(1)} %bitcast.160), kind=kOutput, calls=%fused_computation.18 | convolution fusion | flops 536870912 | bytes 39845888 | tf_op jit(solution)/shard_map/cond/branch_1_fun/fkwi,fwj->fkij/dot_general | solution.py:38
  225.3 43.0 %fusion.21 = f32[1,2,16384]{2,1,0:T(2,128)S(1)} fusion(f32[2,512]{1,0:T(2,128)S(1)} %get-tuple-element.43, f32[64,8,128,128]{3,2,1,0:T(8,128)} %bitcast.159), kind=kOutput, calls=%fused_computation.17 | convolution fusion | flops 201326592 | bytes 33689600 | tf_op jit(solution)/shard_map/cond/branch_1_fun/dot_general | solution.py:42
  268.6 0.9 pad_maximum_fusion.4
  269.6 0.6 dynamic-slice
  270.2 25.0 %all-reduce.3.cloned.1.call-done = f32[3,2,16384]{2,1,0:T(2,128)} async-done(((f32[3,2,16384]{2,1,0:T(2,128)}), f32[3,2,16384]{2,1,0:T(2,128)}) %all-reduce.3.cloned.1.call-update) | async-done | bytes 393232
  295.1 1.9 constant_dynamic-slice_fusion.2
  297.0 3.4 %collective-permute-start.2 = (f32[1,16384]{1,0:T(1,128)S(1)}, f32[1,16384]{1,0:T(1,128)S(1)}, u32[]{:S(2)}, u32[]{:S(2)}) collective-permute-start(f32[1,16384]{1,0:T(1,128)S(1)} %bitcast.166), channel_id=1, source_target_pairs={{0,4},{2,6},{4,8},{6,10},{8,12},{10,14},{12,16},{14,18},{16,20},{1... | collective-permute-start | bytes 196616 | tf_op jit(solution)/shard_map/ppermute | solution.py:17
  300.4 1.9 collective-permute-start.3
  302.3 0.1 copy.91
  302.4 0.1 copy.92
  302.5 0.1 copy.93
  302.6 1.4 collective-permute-done.2
  304.1 2.8 collective-permute-done.3
  306.9 0.9 copy.94
  (27 shorter events, 0.6 us)
Async XLA Ops:
  6.5 288.6 %all-reduce.3.cloned.1.call-start = ((), (), s32[]{:S(2)}) async-start(), calls=%async_computation.1 | async-start | bytes 786432
  68.9 7.0 %copy-start = (s32[16]{0:T(128)S(1)}, s32[16]{0:T(128)}, u32[]{:S(2)}) copy-start(s32[16]{0:T(128)} %param.11) | copy-start | bytes 196
  70.8 73.9 %collective-permute-start = (bf16[2,256,16,128]{3,1,0,2:T(8,128)(2,1)}, bf16[2,256,16,128]{3,1,0,2:T(8,128)(2,1)}, u32[]{:S(2)}, u32[]{:S(2)}) collective-permute-start(bf16[2,256,16,128]{3,1,0,2:T(8,128)(2,1)} %fusion.28), channel_id=1, source_target_pairs={{2,0},{4,2},{6,4},{8,6},{10,8},{12,10},{14,12},{16,14},{18,16},{20... | collective-permute-start | bytes 6291464 | tf_op jit(solution)/shard_map/ppermute | solution.py:17
  73.3 74.8 %collective-permute-start.1 = (bf16[2,256,16,128]{3,1,0,2:T(8,128)(2,1)}, bf16[2,256,16,128]{3,1,0,2:T(8,128)(2,1)}, u32[]{:S(2)}, u32[]{:S(2)}) collective-permute-start(bf16[2,256,16,128]{3,1,0,2:T(8,128)(2,1)} %fusion.28), channel_id=1, source_target_pairs={{4,0},{6,2},{8,4},{10,6},{12,8},{14,10},{16,12},{18,14},{20,16},{2... | collective-permute-start | bytes 6291464 | tf_op jit(solution)/shard_map/ppermute | solution.py:17
  209.3 60.3 %copy-start.1 = (u32[32]{0:T(128)S(1)}, u32[32]{0:T(128)}, u32[]{:S(2)}) copy-start(u32[32]{0:T(128)} %constant.41) | copy-start | bytes 388
  297.0 7.1 %collective-permute-start.2 = (f32[1,16384]{1,0:T(1,128)S(1)}, f32[1,16384]{1,0:T(1,128)S(1)}, u32[]{:S(2)}, u32[]{:S(2)}) collective-permute-start(f32[1,16384]{1,0:T(1,128)S(1)} %bitcast.166), channel_id=1, source_target_pairs={{0,4},{2,6},{4,8},{6,10},{8,12},{10,14},{12,16},{14,18},{16,20},{1... | collective-permute-start | bytes 196616 | tf_op jit(solution)/shard_map/ppermute | solution.py:17
  300.4 6.5 %collective-permute-start.3 = (f32[1,16384]{1,0:T(1,128)S(1)}, f32[1,16384]{1,0:T(1,128)S(1)}, u32[]{:S(2)}, u32[]{:S(2)}) collective-permute-start(f32[1,16384]{1,0:T(1,128)S(1)} %bitcast.164), channel_id=1, source_target_pairs={{0,2},{2,4},{4,6},{6,8},{8,10},{10,12},{12,14},{14,16},{16,18},{18... | collective-permute-start | bytes 196616 | tf_op jit(solution)/shard_map/ppermute | solution.py:17
Sparse Core Ops, SparseCore 0:
  269.7 25.3 all-reduce.2
